TPU v7x, 32 devices: a whole 2x2x4 slice. The times are simulated.
32 devices in a mesh: vx: 2 (over x), vy: 4 (over y, core), scan: 4 (over z).
Axes of the slice: x: 2, y: 2, z: 4, core: 2. Of those that a mesh axis runs over, the one named last changes fastest.
Arguments:
- volume: bfloat16 [2, 64, 256, 256], P(None, 'vx', 'vy'), may hold values from -6 to 6
- tile_matrix: bfloat16 [4, 2, 8, 1024, 128], P('scan', 'vx', 'vy'), may hold values from -0.09375 to 0.09375
- tile_offset: int32 [4, 2, 8], P('scan', 'vx', 'vy'), may hold values from 0 to 384
- patch_count: int32 [4, 8], P('scan', ('vx', 'vy')), may hold values from 1 to 3, as said below
- scan_position: int32 [4, 8, 3, 2], P('scan', ('vx', 'vy')), may hold values from 0 to 256, as said below
- measured: float32 [4, 8, 3, 256, 256], P('scan', ('vx', 'vy')), may hold values from 0.2 to 5
- illumination: float32 [2, 256, 256], replicated, may hold values from -6 to 6
Outputs:
- change: float32 [2, 64, 256, 256], P(None, 'vx', 'vy', 'scan')
Inputs may be any that keep to these rules, and one draw needn't show every extreme that they name: `patch_count`: an owner's slots below its count hold measured patches, the others are unused; at every angle some owner holds 3. `scan_position`: column 0 is a patch's first detector column, 0 to 256; column 1 its first row, 0 to 0.
All inputs are finite; a program needn't handle non-finite values.
Results may differ from a plain program's by a relative error of at most 0.0085.
Values may be sent and summed in bfloat16 or wider, within the bound.
No kernel may reach another device: no remote copies, remote signals or barrier semaphores. Data moves between devices by JAX's collectives and lax.ppermute only.
A program may use at most 64 MiB of HBM per device.

v0:
```python
import math
import jax
import jax.numpy as jnp
from jax import lax
from jax.sharding import PartitionSpec as P

TILE = 32
NZ = 256
U = 512
TU = 128
PATCH_SIDE = 256
ABSORPTION = 0.2
STEP_LENGTH = 0.003


def dft_tables(length):
    counter = jnp.arange(length, dtype=jnp.int32)
    product = counter[:, None] * counter[None, :] % length
    radians = product.astype(jnp.float32) * (2.0 * math.pi / length)
    scaling = 1.0 / math.sqrt(length)
    return (jnp.cos(radians) * scaling, jnp.sin(radians) * scaling)


def matmul(left, right):
    return jnp.dot(left, right, precision=lax.Precision.HIGHEST)


def patch_misfit(window, illumination, intensity, cosine_table, sine_table):
    amplitude = jnp.exp(-ABSORPTION * window[1])
    trans_re = amplitude * jnp.cos(window[0])
    trans_im = amplitude * jnp.sin(window[0])
    exit_re = illumination[0] * trans_re - illumination[1] * trans_im
    exit_im = illumination[0] * trans_im + illumination[1] * trans_re
    half_re = matmul(cosine_table, exit_re) + matmul(sine_table, exit_im)
    half_im = matmul(cosine_table, exit_im) - matmul(sine_table, exit_re)
    far_re = matmul(half_re, cosine_table) + matmul(half_im, sine_table)
    far_im = matmul(half_im, cosine_table) - matmul(half_re, sine_table)
    residue = far_re * far_re + far_im * far_im - intensity
    return jnp.sum(residue * residue)


def place_patch(summed_total, slope, corner):
    anchor = (jnp.zeros((), jnp.int32), corner[0], corner[1])
    before = lax.dynamic_slice(summed_total, anchor, slope.shape)
    return lax.dynamic_update_slice(summed_total, before + slope, anchor)


def patch_term(
    summed_total, projected_field, corner, intensity, illumination, cosine_table, sine_table
):
    anchor = (jnp.zeros((), jnp.int32), corner[0], corner[1])
    window = lax.dynamic_slice(projected_field, anchor, (2, PATCH_SIDE, PATCH_SIDE))
    slope = jax.grad(patch_misfit)(window, illumination, intensity, cosine_table, sine_table)
    return place_patch(summed_total, slope, corner)


def brick_tiles(field):
    components, width_x, width_y, depth_cells = field.shape
    blocks = field.reshape(components, width_x // TILE, TILE, width_y // TILE, TILE, depth_cells)
    blocks = blocks.transpose(1, 3, 0, 2, 4, 5)
    return blocks.reshape(-1, components, TILE * TILE, depth_cells)


def tiles_brick(blocks, width_x, width_y):
    components = blocks.shape[1]
    depth_cells = blocks.shape[3]
    shaped = blocks.reshape(width_x // TILE, width_y // TILE, components, TILE, TILE, depth_cells)
    return shaped.transpose(2, 0, 3, 1, 4, 5).reshape(components, width_x, width_y, depth_cells)


def partial_projection(current, matrices, offsets):
    blocks = brick_tiles(current)
    tile_parts = jnp.einsum("tku,tckz->tcuz", matrices, blocks, preferred_element_type=jnp.float32)
    summed_total = jnp.zeros((2, U, NZ), jnp.float32)
    for tile_index in range(tile_parts.shape[0]):
        anchor = (jnp.zeros((), jnp.int32), offsets[tile_index], jnp.zeros((), jnp.int32))
        before = lax.dynamic_slice(summed_total, anchor, tile_parts.shape[1:])
        summed_total = lax.dynamic_update_slice(
            summed_total, before + tile_parts[tile_index], anchor
        )
    return summed_total


def cut_windows(image, offsets):

    def cut_window(offset):
        anchor = (jnp.zeros((), jnp.int32), offset, jnp.zeros((), jnp.int32))
        return lax.dynamic_slice(image, anchor, (2, TU, NZ))

    return jax.vmap(cut_window)(offsets)


def back_tiles(matrices, windows, width_x, width_y):
    blocks = jnp.einsum("tku,tcuz->tckz", matrices, windows, preferred_element_type=jnp.float32)
    return tiles_brick(blocks, width_x, width_y)


def per_device(
    volume, tile_matrix, tile_offset, patch_count, scan_position, measured, illumination
):
    cosine_table, sine_table = dft_tables(PATCH_SIDE)
    matrices = tile_matrix[0].reshape(-1, TILE * TILE, TU)
    offsets = tile_offset[0].reshape(-1)
    live_count = patch_count[0, 0]
    positions = scan_position[0, 0]
    intensity_values = measured[0, 0]
    width_x = volume.shape[1]
    width_y = volume.shape[2]
    slab_depth = NZ // lax.axis_size("scan")
    slab_start = lax.axis_index("scan") * slab_depth

    def own_slot(slot_index, running, projected_field):
        return patch_term(
            running,
            projected_field,
            positions[slot_index],
            intensity_values[slot_index],
            illumination,
            cosine_table,
            sine_table,
        )

    iterate = lax.dynamic_slice_in_dim(volume, slab_start, slab_depth, 3).astype(jnp.float32)
    projected_field = lax.psum(partial_projection(volume, matrices, offsets), ("vx", "vy"))
    image = lax.psum(
        lax.fori_loop(
            0,
            live_count,
            lambda slot_index, running: own_slot(slot_index, running, projected_field),
            jnp.zeros_like(projected_field),
        ),
        ("vx", "vy"),
    )
    windows = cut_windows(image, offsets).astype(jnp.bfloat16)
    slope = back_tiles(matrices, windows, width_x, width_y)
    slope_sum = lax.psum_scatter(
        slope.astype(jnp.bfloat16), "scan", scatter_dimension=3, tiled=True
    ).astype(jnp.float32)
    iterate = iterate - STEP_LENGTH * slope_sum
    return iterate - lax.dynamic_slice_in_dim(volume, slab_start, slab_depth, 3).astype(jnp.float32)


def solution(mesh):
    in_specs = (
        P(None, "vx", "vy", None),
        P("scan", "vx", "vy", None, None),
        P("scan", "vx", "vy"),
        P("scan", ("vx", "vy")),
        P("scan", ("vx", "vy"), None, None),
        P("scan", ("vx", "vy"), None, None, None),
        P(),
    )
    out_specs = P(None, "vx", "vy", "scan")
    return jax.shard_map(
        per_device, mesh=mesh, in_specs=in_specs, out_specs=out_specs, check_vma=False
    )
```

profile of v0, /device:TPU:0, one launch (start us, length us, event | category | flops | bytes accessed | tf_op | source)
XLA Modules:
  0.0 327.8 jit_solution(10603027786342075903)
XLA Ops:
  6.5 1.3 fusion.124
  10.4 1.8 copy.25
  14.7 1.6 dynamic_update_slice.10
  16.5 1.6 dynamic_update_slice.11
  19.4 59.3 %all-reduce.6.cloned.1.call-done = f32[2,512,256]{1,2,0:T(8,128)} async-done(((f32[2,512,256]{1,2,0:T(8,128)}), f32[2,512,256]{1,2,0:T(8,128)}) %all-reduce.6.cloned.1.call-update) | async-done | bytes 1048592 | tf_op jit(solution)/shard_map/psum | solution.py:124
  79.9 51.8 %while.12 = (s32[]{:T(128)}, f32[2,512,256]{2,0,1:T(2,128)}, s32[]{:T(128)}, s32[3,2]{0,1:T(2,128)S(1)}, f32[2,512,256]{1,2,0:T(8,128)}, /*index=5*/f32[2,256,25...) while((s32[]{:T(128)}, f32[2,512,256]{2,0,1:T(2,128)}, ...), condition=%wide.region_2.3_spmd.clone.clone, body=%wide.region_1.2_spmd.clone.clone.sunk | while | flops 3240427520 | bytes 30671164 | solution.py:126
  101.0 2.2 fusion.184
  103.2 1.4 fusion.185
  104.6 1.4 convolution_subtract_fusion.4
  106.0 1.5 fusion.186
  107.4 1.4 fusion.187
  108.8 1.4 convolution_add_fusion.9
  110.2 1.5 convolution_subtract_fusion.5
  111.7 1.5 fusion.188
  113.1 2.4 add_multiply_fusion.3
  115.6 1.4 fusion.191
  117.0 1.4 convolution_add_fusion.11
  118.3 1.4 fusion.189
  119.7 1.4 convolution_add_fusion.10
  121.1 1.5 fusion.190
  122.6 1.5 fusion.192
  124.1 1.5 fusion.193
  125.5 2.4 fusion.194
  131.7 112.3 %all-reduce.7 = bf16[2,512,256]{2,0,1:T(2,128)(2,1)S(1)} all-reduce(f32[2,512,256]{2,0,1:T(2,128)} %get-tuple-element.94), channel_id=1, replica_groups=mesh['vx'=2,'vy'=4,'scan'=4] {'vx','vy'}, use_global_device_ids=true, to_apply=%region_3.4 | all-reduce | flops 262144 | bytes 1572864 | tf_op jit(solution)/shard_map/psum | solution.py:125
  245.9 2.6 copy.30
  248.5 1.8 copy.31
  250.3 6.7 %copy.34 = bf16[2,32,64,256]{2,1,0,3:T(8,128)(2,1)} copy(bf16[2,32,64,256]{3,2,1,0:T(8,128)(2,1)S(1)} %bitcast.209) | data formatting | bytes 4194304
  257.0 6.6 %reshape.60 = bf16[256,4096]{1,0:T(8,128)(2,1)} reshape(bf16[256,2,32,64]{3,2,1,0:T(8,128)(2,1)} %bitcast.208) | data formatting | bytes 4194304
  263.6 48.2 %reduce-scatter.4.cloned.1.call-done = bf16[64,4096]{1,0:T(8,128)(2,1)} async-done(((bf16[256,4096]{1,0:T(8,128)(2,1)}), bf16[64,4096]{1,0:T(8,128)(2,1)}) %reduce-scatter.4.cloned.1.call-update) | async-done | bytes 524304
  311.8 2.7 reshape.61
  314.6 2.9 copy.35
  317.5 3.1 subtract_subtract_fusion
  (37 shorter events, 9.1 us)
Async XLA Ops:
  6.5 5.7 %copy-start = (bf16[1,1,2,1024,128]{4,3,2,1,0:T(8,128)(2,1)S(1)}, bf16[1,1,2,1024,128]{4,3,2,1,0:T(8,128)(2,1)}, u32[]{:S(2)}) copy-start(bf16[1,1,2,1024,128]{4,3,2,1,0:T(8,128)(2,1)} %param.10) | copy-start | bytes 1572868
  6.5 72.2 %all-reduce.6.cloned.1.call-start = ((), (), s32[]{:S(2)}) async-start(), calls=%async_computation.1 | async-start | bytes 2097152 | tf_op jit(solution)/shard_map/psum | solution.py:124
  13.2 6.0 %copy-start.5 = (f32[2,256,256]{2,1,0:T(8,128)S(1)}, f32[2,256,256]{2,1,0:T(8,128)}, u32[]{:S(2)}) copy-start(f32[2,256,256]{2,1,0:T(8,128)} %param.15) | copy-start | bytes 1572868
  14.7 4.7 %copy-start.7 = (s32[1,1,2]{2,1,0:T(1,128)S(1)}, s32[1,1,2]{2,1,0:T(1,128)}, u32[]{:S(2)}) copy-start(s32[1,1,2]{2,1,0:T(1,128)} %param.11) | copy-start | bytes 28
  16.3 63.6 %copy-start.6 = (s32[1,1,3,2]{2,3,1,0:T(2,128)S(1)}, s32[1,1,3,2]{2,3,1,0:T(2,128)}, u32[]{:S(2)}) copy-start(s32[1,1,3,2]{2,3,1,0:T(2,128)} %param.13) | copy-start | bytes 76
  18.1 1.0 copy-start.3
  19.1 292.7 %reduce-scatter.4.cloned.1.call-start = ((), (), s32[]{:S(2)}) async-start(), calls=%async_computation.2 | async-start | bytes 2621440
  121.1 4.4 %copy-start.1 = (f32[2,512,256]{1,2,0:T(8,128)S(1)}, f32[2,512,256]{1,2,0:T(8,128)}, u32[]{:S(2)}) copy-start(f32[2,512,256]{1,2,0:T(8,128)} %get-tuple-element.294) | copy-start | bytes 3145732 | tf_op jit(solution)/shard_map/while
  125.5 3.6 %copy-start.2 = (f32[2,512,256]{2,0,1:T(2,128)S(1)}, f32[2,512,256]{2,0,1:T(2,128)}, u32[]{:S(2)}) copy-start(f32[2,512,256]{2,0,1:T(2,128)} %get-tuple-element.279) | copy-start | bytes 3145732 | tf_op jit(solution)/shard_map/while
  263.6 53.9 %copy-start.4 = (bf16[2,32,64,256]{3,2,1,0:T(8,128)(2,1)S(1)}, bf16[2,32,64,256]{3,2,1,0:T(8,128)(2,1)}, u32[]{:S(2)}) copy-start(bf16[2,32,64,256]{3,2,1,0:T(8,128)(2,1)} %param.9) | copy-start | bytes 6291460
Sparse Core Ops, SparseCore 0:
  19.2 59.4 all-reduce.5
  263.7 48.0 reduce-scatter.3
where the time goes:
time: 331 us; the launch traced here: 328 us
  blocking collectives  112 us (34%)
  waiting for transfers between devices  107 us (32%)
  local copies, waits for them, and re-layouts  35.6 us (11%)
  matrix products  26.3 us (8%)
  loops' own time  21.5 us (6%)
  between operations  17.9 us (5%)
  other arithmetic  6.69 us (2%)
    psum x1, blocking collectives, per_device(): lax.psum(lax.fori_loop(0, live_count, lambda slot_index, running: own_slo...  112 us
    psum x1, waiting for transfers between devices, per_device(): lax.psum(partial_projection(volume, matrices, offsets), ('vx', 'vy'))  59.3 us
    unnamed x3, waiting for transfers between devices  48.2 us
    dot_general x16, matrix products, matmul(): return jnp.dot(left, right, precision=lax.Precision.HIGHEST)  24.6 us
    another operation x1, loops' own time, per_device(): lax.fori_loop(0, live_count, lambda slot_index, running: own_slot(slot_in...  21.5 us
    unnamed x17, local copies, waits for them, and re-layouts  20.1 us
  transfers between devices with their start and end apart: 2, of which 2 were waited for; matrix products, arithmetic and copies ran while one was open for 0% of the time, Pallas kernels for 0%

commit v1 on v0

--- a/solution.py
+++ b/solution.py
@@ -3,6 +3,7 @@
 import jax.numpy as jnp
 from jax import lax
 from jax.sharding import PartitionSpec as P
+from jax.lax import psum
 
 TILE = 32
 NZ = 256
@@ -11,6 +12,12 @@
 PATCH_SIDE = 256
 ABSORPTION = 0.2
 STEP_LENGTH = 0.003
+
+
+def step_on_the_terms(unit):
+    for rr in ("vy", "vx"):
+        unit = psum(unit, rr)
+    return unit
 
 
 def dft_tables(length):
@@ -122,14 +129,13 @@
 
     iterate = lax.dynamic_slice_in_dim(volume, slab_start, slab_depth, 3).astype(jnp.float32)
     projected_field = lax.psum(partial_projection(volume, matrices, offsets), ("vx", "vy"))
-    image = lax.psum(
+    image = step_on_the_terms(
         lax.fori_loop(
             0,
             live_count,
             lambda slot_index, running: own_slot(slot_index, running, projected_field),
             jnp.zeros_like(projected_field),
-        ),
-        ("vx", "vy"),
+        )
     )
     windows = cut_windows(image, offsets).astype(jnp.bfloat16)
     slope = back_tiles(matrices, windows, width_x, width_y)

time: 331 us -> 345 us (1.042)
  waiting for transfers between devices: 107 us -> 205 us
  blocking collectives: 112 us -> 28.5 us
    psum x0 -> x1, waiting for transfers between devices: none -> 102 us  [step_on_the_terms(): unit = psum(unit, rr)]
    psum x1, blocking collectives: 112 us -> 28.5 us  [step_on_the_terms(): unit = psum(unit, rr)]
    unnamed x3 -> x4, waiting for transfers between devices: 48.2 us -> 44.1 us
  transfers between devices with their start and end apart: 2 -> 3, of which waited for: 2 -> 3; matrix products, arithmetic and copies ran while one was open for 0% -> 0% of each run, Pallas kernels for 0% -> 0%
where the time goes in v1:
time: 345 us; the launch traced here: 341 us
  waiting for transfers between devices  205 us (59%)
  local copies, waits for them, and re-layouts  35.6 us (10%)
  blocking collectives  28.5 us (8%)
  matrix products  26.3 us (8%)
  loops' own time  21.5 us (6%)
  between operations  17.6 us (5%)
  other arithmetic  6.69 us (2%)
    psum x1, waiting for transfers between devices, step_on_the_terms(): unit = psum(unit, rr)  102 us
    psum x1, waiting for transfers between devices, per_device(): lax.psum(partial_projection(volume, matrices, offsets), ('vx', 'vy'))  59.3 us
    unnamed x4, waiting for transfers between devices  44.1 us
    psum x1, blocking collectives, step_on_the_terms(): unit = psum(unit, rr)  28.5 us
    dot_general x16, matrix products, matmul(): return jnp.dot(left, right, precision=lax.Precision.HIGHEST)  24.6 us
    another operation x1, loops' own time, per_device(): lax.fori_loop(0, live_count, lambda slot_index, running: own_slot(slot_in...  21.5 us
    unnamed x17, local copies, waits for them, and re-layouts  20.1 us
  transfers between devices with their start and end apart: 3, of which 3 were waited for; matrix products, arithmetic and copies ran while one was open for 0% of the time, Pallas kernels for 0%

profile of v1, /device:TPU:0, one launch (start us, length us, event | category | flops | bytes accessed | tf_op | source)
XLA Modules:
  0.0 341.2 jit_solution(16040897933049914428)
XLA Ops:
  10.4 1.8 copy.25
  14.7 1.6 dynamic_update_slice.10
  16.5 1.6 dynamic_update_slice.11
  19.4 59.3 %all-reduce.7.cloned.1.call-done = f32[2,512,256]{1,2,0:T(8,128)} async-done(((f32[2,512,256]{1,2,0:T(8,128)}), f32[2,512,256]{1,2,0:T(8,128)}) %all-reduce.7.cloned.1.call-update) | async-done | bytes 1048592 | tf_op jit(solution)/shard_map/psum | solution.py:131
  79.9 51.8 %while.12 = (s32[]{:T(128)}, f32[2,512,256]{2,0,1:T(2,128)}, s32[]{:T(128)}, s32[3,2]{0,1:T(2,128)S(1)}, f32[2,512,256]{1,2,0:T(8,128)}, /*index=5*/f32[2,256,25...) while((s32[]{:T(128)}, f32[2,512,256]{2,0,1:T(2,128)}, ...), condition=%wide.region_2.3_spmd.clone.clone, body=%wide.region_1.2_spmd.clone.clone.sunk | while | flops 3240427520 | bytes 30671164 | solution.py:133
  101.0 2.2 fusion.184
  103.2 1.4 fusion.185
  104.6 1.4 convolution_subtract_fusion.4
  106.0 1.5 fusion.186
  107.5 1.4 fusion.187
  108.8 1.4 convolution_add_fusion.9
  110.2 1.5 convolution_subtract_fusion.5
  111.7 1.5 fusion.188
  113.1 2.4 add_multiply_fusion.3
  115.6 1.4 fusion.191
  117.0 1.4 convolution_add_fusion.11
  118.3 1.4 fusion.189
  119.7 1.4 convolution_add_fusion.10
  121.1 1.5 fusion.190
  122.6 1.5 fusion.192
  124.1 1.5 fusion.193
  125.6 2.4 fusion.194
  131.8 101.6 %all-reduce.9.cloned.1.call-done = f32[2,512,256]{2,0,1:T(2,128)} async-done(((f32[2,512,256]{2,0,1:T(2,128)}), f32[2,512,256]{2,0,1:T(2,128)}) %all-reduce.9.cloned.1.call-update) | async-done | bytes 1048592 | tf_op jit(solution)/shard_map/psum | solution.py:19
  233.4 28.5 %all-reduce.10 = bf16[2,512,256]{2,0,1:T(2,128)(2,1)S(1)} all-reduce(f32[2,512,256]{2,0,1:T(2,128)} %all-reduce.9.cloned.1.call-done), channel_id=1, replica_groups=mesh['vx'=2,'vy'=4,'scan'=4] {'vx'}, use_global_device_ids=true, to_apply=%region_4.5 | all-reduce | flops 262144 | bytes 1572864 | tf_op jit(solution)/shard_map/psum | solution.py:19
  263.8 2.6 copy.30
  266.3 1.8 copy.31
  268.2 6.7 %copy.34 = bf16[2,32,64,256]{2,1,0,3:T(8,128)(2,1)} copy(bf16[2,32,64,256]{3,2,1,0:T(8,128)(2,1)S(1)} %bitcast.209) | data formatting | bytes 4194304
  274.9 6.6 %reshape.60 = bf16[256,4096]{1,0:T(8,128)(2,1)} reshape(bf16[256,2,32,64]{3,2,1,0:T(8,128)(2,1)} %bitcast.208) | data formatting | bytes 4194304
  281.5 44.1 %reduce-scatter.4.cloned.1.call-done = bf16[64,4096]{1,0:T(8,128)(2,1)} async-done(((bf16[256,4096]{1,0:T(8,128)(2,1)}), bf16[64,4096]{1,0:T(8,128)(2,1)}) %reduce-scatter.4.cloned.1.call-update) | async-done | bytes 524304
  325.6 2.7 reshape.61
  328.3 2.9 copy.35
  331.3 3.1 subtract_subtract_fusion
  (40 shorter events, 10.4 us)
Async XLA Ops:
  6.5 5.7 %copy-start = (bf16[1,1,2,1024,128]{4,3,2,1,0:T(8,128)(2,1)S(1)}, bf16[1,1,2,1024,128]{4,3,2,1,0:T(8,128)(2,1)}, u32[]{:S(2)}) copy-start(bf16[1,1,2,1024,128]{4,3,2,1,0:T(8,128)(2,1)} %param.10) | copy-start | bytes 1572868
  6.5 72.1 %all-reduce.7.cloned.1.call-start = ((), (), s32[]{:S(2)}) async-start(), calls=%async_computation.1 | async-start | bytes 2097152 | tf_op jit(solution)/shard_map/psum | solution.py:131
  13.2 6.0 %copy-start.5 = (f32[2,256,256]{2,1,0:T(8,128)S(1)}, f32[2,256,256]{2,1,0:T(8,128)}, u32[]{:S(2)}) copy-start(f32[2,256,256]{2,1,0:T(8,128)} %param.15) | copy-start | bytes 1572868
  16.3 63.6 %copy-start.6 = (s32[1,1,3,2]{2,3,1,0:T(2,128)S(1)}, s32[1,1,3,2]{2,3,1,0:T(2,128)}, u32[]{:S(2)}) copy-start(s32[1,1,3,2]{2,3,1,0:T(2,128)} %param.13) | copy-start | bytes 76
  18.1 1.0 copy-start.3
  19.1 214.3 %all-reduce.9.cloned.1.call-start = ((), (), s32[]{:S(2)}) async-start(), calls=%async_computation.2 | async-start | bytes 2097152 | tf_op jit(solution)/shard_map/psum | solution.py:19
  79.9 51.9 %copy-start.7 = (s32[1,1,2]{2,1,0:T(1,128)S(1)}, s32[1,1,2]{2,1,0:T(1,128)}, u32[]{:S(2)}) copy-start(s32[1,1,2]{2,1,0:T(1,128)} %param.11) | copy-start | bytes 28
  121.1 4.4 %copy-start.1 = (f32[2,512,256]{1,2,0:T(8,128)S(1)}, f32[2,512,256]{1,2,0:T(8,128)}, u32[]{:S(2)}) copy-start(f32[2,512,256]{1,2,0:T(8,128)} %get-tuple-element.294) | copy-start | bytes 3145732 | tf_op jit(solution)/shard_map/while
  125.5 3.6 %copy-start.2 = (f32[2,512,256]{2,0,1:T(2,128)S(1)}, f32[2,512,256]{2,0,1:T(2,128)}, u32[]{:S(2)}) copy-start(f32[2,512,256]{2,0,1:T(2,128)} %get-tuple-element.279) | copy-start | bytes 3145732 | tf_op jit(solution)/shard_map/while
  131.8 193.8 %reduce-scatter.4.cloned.1.call-start = ((), (), s32[]{:S(2)}) async-start(), calls=%async_computation.3 | async-start | bytes 2621440
  281.5 49.8 %copy-start.4 = (bf16[2,32,64,256]{3,2,1,0:T(8,128)(2,1)S(1)}, bf16[2,32,64,256]{3,2,1,0:T(8,128)(2,1)}, u32[]{:S(2)}) copy-start(bf16[2,32,64,256]{3,2,1,0:T(8,128)(2,1)} %param.9) | copy-start | bytes 6291460
Sparse Core Ops, SparseCore 0:
  19.2 59.4 all-reduce.6
  131.9 101.5 all-reduce.8
  281.6 43.9 reduce-scatter.3
